TPU v7x, 256 devices: a whole 4x4x8 slice. The times are simulated.
256 devices in a mesh: tm: 32 (over z, y), slab: 8 (over x, core).
Axes of the slice: x: 4, y: 4, z: 8, core: 2. Of those that a mesh axis runs over, the one named last changes fastest.
Arguments:
- features: bfloat16 [32, 12288, 256], P('tm', 'slab'), may hold values from -6 to 6
- ref_lists: int32 [32, 8, 32], P('tm'), may hold values from 0 to 11
- tile_rows: int32 [32, 256], P('tm', 'slab'), may hold values from 0 to 11
- tile_sources: int32 [32, 256], P('tm', 'slab'), may hold values from 0 to 31
- tile_counts: int32 [32, 8], P('tm', 'slab'), may hold values from 9 to 32
- tile_values: bfloat16 [32, 256, 128, 128], P('tm', 'slab'), may hold values from -0.3125 to 0.3125
- w_input: bfloat16 [2, 256, 1024], replicated, may hold values from -0.375 to 0.375
- w_hidden: bfloat16 [2, 256, 1024], replicated, may hold values from -0.375 to 0.375
- bias: float32 [2, 1024], replicated, may hold values from -4 to 4
Outputs:
- hidden_out: bfloat16 [32, 12288, 256], P('tm', 'slab')
Inputs may be any that keep to these rules, and one draw needn't show every extreme that they name: `ref_lists`: row tile indices within a slab. `tile_counts`: slots at or after the count are ignored.
All inputs are finite; a program needn't handle non-finite values.
Results may differ from a plain program's by a relative error of at most 0.0055.
Values may be sent and summed in bfloat16 or wider, within the bound.
A program may use at most 64 MiB of HBM per device.

v0:
```python
import jax
import jax.numpy as jnp
from jax import lax
from jax.sharding import PartitionSpec as P


def lstm_run(inputs, weight_in, weight_rec, gate_bias):
    steps_count, vertex_count, feature_width = inputs.shape
    projected = jnp.dot(
        inputs.reshape(-1, feature_width), weight_in, preferred_element_type=jnp.float32
    )
    projected = projected.reshape(steps_count, vertex_count, -1) + gate_bias
    unit_count = weight_rec.shape[0]

    def advance(state, gate_input):
        hidden, memory = state
        gate_sum = gate_input + jnp.dot(hidden, weight_rec, preferred_element_type=jnp.float32)
        in_gate, forget, candidate, out_gate = jnp.split(gate_sum, 4, axis=-1)
        memory = jax.nn.sigmoid(forget) * memory + jax.nn.sigmoid(in_gate) * jnp.tanh(candidate)
        hidden = (jax.nn.sigmoid(out_gate) * jnp.tanh(memory)).astype(jnp.bfloat16)
        return ((hidden, memory), hidden)

    start_state = (
        jnp.zeros((vertex_count, unit_count), jnp.bfloat16),
        jnp.zeros((vertex_count, unit_count), jnp.float32),
    )
    final_state, outputs = lax.scan(advance, start_state, projected, unroll=4)
    return outputs


def local(
    features, ref_lists, tile_rows, tile_sources, tile_counts, tile_values, w_input, w_hidden, bias
):
    current = features[0]
    row_count, feature_width = current.shape
    tile_size = tile_values.shape[2]
    slot_count = tile_values.shape[1]
    row_tiles = row_count // tile_size
    slab_count = lax.axis_size("slab")
    group_count = lax.axis_size("tm")
    slab_index = lax.axis_index("slab")
    ref_table = ref_lists[0]
    list_length = ref_table.shape[1] // slab_count
    weight_tiles = tile_values[0]
    sources = tile_sources[0]
    live = jnp.arange(slot_count, dtype=jnp.int32) < tile_counts[0, 0]
    one_hot = (tile_rows[0][None, :] == jnp.arange(row_tiles, dtype=jnp.int32)[:, None]) & live[
        None, :
    ]
    one_hot = one_hot.astype(jnp.float32)
    for layer_index in range(w_input.shape[0]):
        wanted = lax.dynamic_slice_in_dim(ref_table, slab_index * list_length, list_length, 1)
        own_tiles = current.reshape(row_tiles, tile_size, -1)
        outgoing = jnp.take(own_tiles, wanted.reshape(-1), axis=0).reshape(
            slab_count, list_length, tile_size, -1
        )
        arrived = lax.all_to_all(outgoing, "slab", split_axis=0, concat_axis=0, tiled=True)
        arrived = arrived.reshape(slab_count * list_length, tile_size, -1)
        picked = jnp.take(arrived, sources, axis=0)
        products = jnp.einsum(
            "kij,kjf->kif", weight_tiles, picked, preferred_element_type=jnp.float32
        )
        mixed = jnp.einsum("rk,kif->rif", one_hot, products).astype(jnp.bfloat16)
        grouped = mixed.reshape(group_count, row_count // group_count, -1)

        def recur(vertex_part, layer_index=layer_index):
            states = lstm_run(
                vertex_part, w_input[layer_index], w_hidden[layer_index], bias[layer_index]
            )
            return lax.all_to_all(states, "tm", split_axis=0, concat_axis=0, tiled=True)

        current = recur(
            lax.all_to_all(grouped, "tm", split_axis=0, concat_axis=0, tiled=True)
        ).reshape(row_count, -1)
    return current[None]


def solution(mesh):
    in_specs = (
        P("tm", "slab", None),
        P("tm", None, None),
        P("tm", "slab"),
        P("tm", "slab"),
        P("tm", "slab"),
        P("tm", "slab", None, None),
        P(),
        P(),
        P(),
    )
    out_specs = P("tm", "slab", None)
    return jax.shard_map(local, mesh=mesh, in_specs=in_specs, out_specs=out_specs, check_vma=False)
```

profile of v0, /device:TPU:8, one launch (start us, length us, event | category | flops | bytes accessed | tf_op | source)
XLA Modules:
  0.0 307.8 jit_solution(12780815506039334951)
XLA Ops:
  1.0 3.1 %gather_fusion = bf16[32,128,256]{2,1,0:T(8,128)(2,1)} fusion(bf16[12,128,256]{2,1,0:T(8,128)(2,1)} %bitcast.187, s32[1024]{0:T(1024)S(1)} %pad_clamp_fusion.1), kind=kCustom, calls=%fused_computation.clone | custom fusion | bytes 4194432 | tf_op jit(solution)/shard_map/jit(_take)/gather | solution.py:54
  4.1 3.1 %broadcast_select_fusion = bf16[32,128,256]{2,1,0:T(8,128)(2,1)} fusion(bf16[32,128,256]{2,1,0:T(8,128)(2,1)} %gather_fusion, pred[32]{0:T(512)(128)(4,1)S(1)} %compare_and_fusion.1), kind=kLoop, calls=%fused_computation.188 | loop fusion | flops 1048576 | bytes 4194336 | tf_op jit(solution)/shard_map/jit(_take)/select_n | solution.py:54
  7.2 4.5 %all-to-all-start = ((bf16[8,4,128,256]{3,2,1,0:T(8,128)(2,1)}), bf16[8,4,128,256]{3,2,1,0:T(8,128)(2,1)}, u32[]{:S(2)}, u32[]{:S(2)}) async-start(bf16[8,4,128,256]{3,2,1,0:T(8,128)(2,1)} %bitcast.184), calls=%async_computation | async-start | bytes 4194304 | tf_op jit(solution)/shard_map/all_to_all | solution.py:57
  12.4 26.5 %all-to-all-done = bf16[8,4,128,256]{3,2,1,0:T(8,128)(2,1)} async-done(((bf16[8,4,128,256]{3,2,1,0:T(8,128)(2,1)}), bf16[8,4,128,256]{3,2,1,0:T(8,128)(2,1)}, u32[]{:S(2)}, u32[]{:S(2)}) %all-to-all-start) | async-done | bytes 2097184 | tf_op jit(solution)/shard_map/all_to_all | solution.py:57
  39.0 3.6 %gather_fusion.1 = bf16[32,128,256]{2,1,0:T(8,128)(2,1)} fusion(bf16[32,128,256]{2,1,0:T(8,128)(2,1)} %bitcast.6, s32[1024]{0:T(1024)S(1)} %pad_clamp_fusion), kind=kCustom, calls=%fused_computation.1.clone | custom fusion | bytes 4194432 | tf_op jit(solution)/shard_map/jit(_take)/gather | solution.py:59
  42.6 3.8 %fusion.128 = bf16[32,256,128]{2,1,0:T(8,128)(2,1)} fusion(bf16[32,128,256]{2,1,0:T(8,128)(2,1)} %gather_fusion.1, pred[32]{0:T(512)(128)(4,1)S(1)} %compare_and_fusion, bf16[1,32,128,128]{3,2,1,0:T(8,128)(2,1)S(1)} %copy-done), kind=kOutput, calls=%fused_computation.184 | convolution fusion | flops 269484032 | bytes 5242912 | tf_op jit(solution)/shard_map/kij,kjf->kif/dot_general | solution.py:60
  46.3 4.6 %copy.12 = bf16[32,256,128]{1,0,2:T(8,128)(2,1)} copy(bf16[32,256,128]{2,1,0:T(8,128)(2,1)} %fusion.128) | data formatting | bytes 4194304 | tf_op jit(solution)/shard_map/kij,kjf->kif/dot_general | solution.py:60
  50.9 2.0 fusion.132
  54.0 11.7 %all-to-all-start.1 = ((bf16[32,48,256]{2,1,0:T(8,128)(2,1)}), bf16[32,48,256]{2,1,0:T(8,128)(2,1)S(1)}, u32[]{:S(2)}, u32[]{:S(2)}) async-start(bf16[32,48,256]{2,1,0:T(8,128)(2,1)} %bitcast.194), calls=%async_computation.1 | async-start | bytes 1572864 | tf_op jit(solution)/shard_map/all_to_all | solution.py:73
  67.1 20.9 %all-to-all-done.1 = bf16[32,48,256]{2,1,0:T(8,128)(2,1)S(1)} async-done(((bf16[32,48,256]{2,1,0:T(8,128)(2,1)}), bf16[32,48,256]{2,1,0:T(8,128)(2,1)S(1)}, u32[]{:S(2)}, u32[]{:S(2)}) %all-to-all-start.1) | async-done | bytes 786464 | tf_op jit(solution)/shard_map/all_to_all | solution.py:73
  88.0 4.7 %broadcast_add_fusion.1 = f32[32,48,1024]{2,1,0:T(8,128)} fusion(f32[1024]{0:T(1024)S(1)} %bitcast.201, bf16[32,48,256]{2,1,0:T(8,128)(2,1)S(1)} %all-to-all-done.1, bf16[2,256,1024]{2,1,0:T(8,128)(2,1)} %param.23), kind=kOutput, calls=%fused_computation.181 | convolution fusion | flops 806879232 | bytes 7606272 | tf_op jit(solution)/shard_map/dot_general | solution.py:9
  92.8 39.4 %while.30 = (s32[]{:T(128)}, bf16[48,256]{1,0:T(8,128)(2,1)S(1)}, f32[48,256]{1,0:T(8,128)S(1)}, bf16[8,4,48,256]{3,2,1,0:T(8,128)(2,1)S(1)}, f32[8,4,48,1024]{3...) while((s32[]{:T(128)}, bf16[48,256]{1,0:T(8,128)(2,1)S(1)}, ...), condition=%wide.region_1.0_spmd.clone, body=%wide.region_0.3_spmd.clone.sunk | while | flops 101965824 | bytes 5243068 | solution.py:27
  132.1 26.7 %all_to_all.30 = bf16[32,48,256]{2,1,0:T(8,128)(2,1)S(1)} all-to-all(bf16[32,48,256]{2,1,0:T(8,128)(2,1)S(1)} %bitcast.196), channel_id=1, replica_groups=mesh['tm'=32,'slab'=8] {'tm'}, dimensions={0} | all-to-all | bytes 1572864 | tf_op jit(solution)/shard_map/all_to_all | solution.py:70
  158.8 2.0 gather_fusion.2
  162.7 30.7 %all_to_all.31 = bf16[8,4,128,256]{3,2,1,0:T(8,128)(2,1)} all-to-all(bf16[8,4,128,256]{3,2,1,0:T(8,128)(2,1)S(1)} %bitcast.185), channel_id=1, replica_groups=mesh['tm'=32,'slab'=8] {'slab'}, dimensions={0} | all-to-all | bytes 4194304 | tf_op jit(solution)/shard_map/all_to_all | solution.py:57
  193.4 3.6 %gather_fusion.3 = bf16[32,128,256]{2,1,0:T(8,128)(2,1)} fusion(bf16[32,128,256]{2,1,0:T(8,128)(2,1)} %bitcast.186, s32[1024]{0:T(1024)S(1)} %pad_clamp_fusion), kind=kCustom, calls=%fused_computation.3.clone | custom fusion | bytes 4194432 | tf_op jit(solution)/shard_map/jit(_take)/gather | solution.py:59
  197.0 3.7 %fusion.126 = bf16[32,256,128]{2,1,0:T(8,128)(2,1)} fusion(bf16[32,128,256]{2,1,0:T(8,128)(2,1)} %gather_fusion.3, pred[32]{0:T(512)(128)(4,1)S(1)} %compare_and_fusion, bf16[1,32,128,128]{3,2,1,0:T(8,128)(2,1)S(1)} %copy-done), kind=kOutput, calls=%fused_computation.182 | convolution fusion | flops 269484032 | bytes 5242912 | tf_op jit(solution)/shard_map/kij,kjf->kif/dot_general | solution.py:60
  200.7 4.6 %copy.13 = bf16[32,256,128]{1,0,2:T(8,128)(2,1)} copy(bf16[32,256,128]{2,1,0:T(8,128)(2,1)} %fusion.126) | data formatting | bytes 4194304 | tf_op jit(solution)/shard_map/kij,kjf->kif/dot_general | solution.py:60
  205.3 2.0 fusion.135
  208.5 5.6 %all-to-all-start.4 = ((bf16[32,48,256]{2,1,0:T(8,128)(2,1)}), bf16[32,48,256]{2,1,0:T(8,128)(2,1)S(1)}, u32[]{:S(2)}, u32[]{:S(2)}) async-start(bf16[32,48,256]{2,1,0:T(8,128)(2,1)} %bitcast.20), calls=%async_computation.4 | async-start | bytes 1572864 | tf_op jit(solution)/shard_map/all_to_all | solution.py:73
  214.0 22.1 %all-to-all-done.4 = bf16[32,48,256]{2,1,0:T(8,128)(2,1)S(1)} async-done(((bf16[32,48,256]{2,1,0:T(8,128)(2,1)}), bf16[32,48,256]{2,1,0:T(8,128)(2,1)S(1)}, u32[]{:S(2)}, u32[]{:S(2)}) %all-to-all-start.4) | async-done | bytes 786464 | tf_op jit(solution)/shard_map/all_to_all | solution.py:73
  236.1 4.7 %broadcast_add_fusion = f32[32,48,1024]{2,1,0:T(8,128)} fusion(f32[1024]{0:T(1024)S(1)} %bitcast.200, bf16[32,48,256]{2,1,0:T(8,128)(2,1)S(1)} %all-to-all-done.4, bf16[2,256,1024]{2,1,0:T(8,128)(2,1)} %param.23), kind=kOutput, calls=%fused_computation.180 | convolution fusion | flops 806879232 | bytes 7606272 | tf_op jit(solution)/shard_map/dot_general | solution.py:9
  240.9 39.4 %while.31 = (s32[]{:T(128)}, bf16[48,256]{1,0:T(8,128)(2,1)S(1)}, f32[48,256]{1,0:T(8,128)S(1)}, bf16[8,4,48,256]{3,2,1,0:T(8,128)(2,1)S(1)}, f32[8,4,48,1024]{3...) while((s32[]{:T(128)}, bf16[48,256]{1,0:T(8,128)(2,1)S(1)}, ...), condition=%wide.region_3.6_spmd.clone, body=%wide.region_2.5_spmd.clone.sunk | while | flops 101965824 | bytes 5243068 | solution.py:27
  280.3 26.7 %all_to_all.32 = bf16[32,48,256]{2,1,0:T(8,128)(2,1)S(1)} all-to-all(bf16[32,48,256]{2,1,0:T(8,128)(2,1)S(1)} %bitcast.195), channel_id=1, replica_groups=mesh['tm'=32,'slab'=8] {'tm'}, dimensions={0} | all-to-all | bytes 1572864 | tf_op jit(solution)/shard_map/all_to_all | solution.py:70
  (173 shorter events, 84.9 us)
Async XLA Ops:
  0.0 42.6 %copy-start = (bf16[1,32,128,128]{3,2,1,0:T(8,128)(2,1)S(1)}, bf16[1,32,128,128]{3,2,1,0:T(8,128)(2,1)}, u32[]{:S(2)}) copy-start(bf16[1,32,128,128]{3,2,1,0:T(8,128)(2,1)} %param.22) | copy-start | bytes 3145732
  7.2 5.1 %copy-start.3 = (s32[1,32]{1,0:T(1,128)S(1)}, s32[1,32]{1,0:T(1,128)}, u32[]{:S(2)}) copy-start(s32[1,32]{1,0:T(1,128)} %param.20) | copy-start | bytes 388
  7.2 31.7 %all-to-all-start = ((bf16[8,4,128,256]{3,2,1,0:T(8,128)(2,1)}), bf16[8,4,128,256]{3,2,1,0:T(8,128)(2,1)}, u32[]{:S(2)}, u32[]{:S(2)}) async-start(bf16[8,4,128,256]{3,2,1,0:T(8,128)(2,1)} %bitcast.184), calls=%async_computation | async-start | bytes 4194304 | tf_op jit(solution)/shard_map/all_to_all | solution.py:57
  46.3 4.6 %copy-start.2 = (s32[1,32]{1,0:T(1,128)S(1)}, s32[1,32]{1,0:T(1,128)}, u32[]{:S(2)}) copy-start(s32[1,32]{1,0:T(1,128)} %param.19) | copy-start | bytes 388
  52.9 12.9 %copy-start.1 = (f32[2,1024]{1,0:T(2,128)S(1)}, f32[2,1024]{1,0:T(2,128)}, u32[]{:S(2)}) copy-start(f32[2,1024]{1,0:T(2,128)} %param.25) | copy-start | bytes 24580
  54.0 34.0 %all-to-all-start.1 = ((bf16[32,48,256]{2,1,0:T(8,128)(2,1)}), bf16[32,48,256]{2,1,0:T(8,128)(2,1)S(1)}, u32[]{:S(2)}, u32[]{:S(2)}) async-start(bf16[32,48,256]{2,1,0:T(8,128)(2,1)} %bitcast.194), calls=%async_computation.1 | async-start | bytes 1572864 | tf_op jit(solution)/shard_map/all_to_all | solution.py:73
  208.5 27.7 %all-to-all-start.4 = ((bf16[32,48,256]{2,1,0:T(8,128)(2,1)}), bf16[32,48,256]{2,1,0:T(8,128)(2,1)S(1)}, u32[]{:S(2)}, u32[]{:S(2)}) async-start(bf16[32,48,256]{2,1,0:T(8,128)(2,1)} %bitcast.20), calls=%async_computation.4 | async-start | bytes 1572864 | tf_op jit(solution)/shard_map/all_to_all | solution.py:73
where the time goes:
time: 310 us; the launch traced here: 308 us
  matrix products  93.7 us (30%)
  blocking collectives  84.1 us (27%)
  waiting for transfers between devices  69.5 us (22%)
  local copies, waits for them, and re-layouts  27 us (9%)
  starting transfers between devices  21.7 us (7%)
  other arithmetic  9.77 us (3%)
    dot_general x64, matrix products, advance(): jnp.dot(hidden, weight_rec, preferred_element_type=jnp.float32)  72.8 us
    all_to_all x2, blocking collectives, recur(): return lax.all_to_all(states, 'tm', split_axis=0, concat_axis=0, tiled=True)  53.4 us
    all_to_all x2, waiting for transfers between devices, local(): lax.all_to_all(grouped, 'tm', split_axis=0, concat_axis=0, tiled=True)  43 us
    all_to_all x1, blocking collectives, local(): lax.all_to_all(outgoing, 'slab', split_axis=0, concat_axis=0, tiled=True)  30.7 us
    all_to_all x1, waiting for transfers between devices, local(): lax.all_to_all(outgoing, 'slab', split_axis=0, concat_axis=0, tiled=True)  26.5 us
    all_to_all x2, starting transfers between devices, local(): lax.all_to_all(grouped, 'tm', split_axis=0, concat_axis=0, tiled=True)  17.3 us
    dot_general x2, matrix products, lstm_run(): jnp.dot(inputs.reshape(-1, feature_width), weight_in, preferred_element_t...  9.38 us
    dot_general x2, local copies, waits for them, and re-layouts, local(): jnp.einsum('kij,kjf->kif', weight_tiles, picked, preferred_element_type=j...  9.17 us
  transfers between devices with their start and end apart: 3, of which 3 were waited for; matrix products, arithmetic and copies ran while one was open for 0% of the time, Pallas kernels for 0%

commit v1 on v0

--- a/solution.py
+++ b/solution.py
@@ -2,6 +2,22 @@
 import jax.numpy as jnp
 from jax import lax
 from jax.sharding import PartitionSpec as P
+
+
+def swapped_with_each(array, axis, split, join):
+    ways, here = (lax.axis_size(axis), lax.axis_index(axis))
+    width = array.shape[split] // ways
+    shape = list(array.shape)
+    shape[split] = width
+    height = shape[join]
+    shape[join] = height * ways
+    full = jnp.zeros(shape, array.dtype)
+    for mask in range(ways):
+        part = lax.dynamic_slice_in_dim(array, (here ^ mask) * width, width, axis=split)
+        if mask:
+            part = lax.ppermute(part, axis, [(d, d ^ mask) for d in range(ways)])
+        full = lax.dynamic_update_slice_in_dim(full, part, (here ^ mask) * height, axis=join)
+    return full
 
 
 def lstm_run(inputs, weight_in, weight_rec, gate_bias):
@@ -54,7 +70,7 @@
         outgoing = jnp.take(own_tiles, wanted.reshape(-1), axis=0).reshape(
             slab_count, list_length, tile_size, -1
         )
-        arrived = lax.all_to_all(outgoing, "slab", split_axis=0, concat_axis=0, tiled=True)
+        arrived = swapped_with_each(outgoing, "slab", 0, 0)
         arrived = arrived.reshape(slab_count * list_length, tile_size, -1)
         picked = jnp.take(arrived, sources, axis=0)
         products = jnp.einsum(

time: 310 us -> 314 us (1.013)
  blocking collectives: 84.1 us -> 54 us
  starting transfers between devices: 21.7 us -> 36.1 us
  local copies, waits for them, and re-layouts: 27 us -> 39.5 us
  waiting for transfers between devices: 69.5 us -> 79.6 us
  matrix products: 93.7 us -> 90.5 us
    ppermute x0 -> x14, waiting for transfers between devices: none -> 35.3 us  [swapped_with_each(): part = lax.ppermute(part, axis, [(d, d ^ mask) for d in range(ways)])]
    all_to_all x1 -> x0, blocking collectives: 30.7 us -> none  [local(): lax.all_to_all(outgoing, 'slab', split_axis=0, concat_axis=0, tiled=True)]
    all_to_all x1 -> x0, waiting for transfers between devices: 26.5 us -> none  [local(): lax.all_to_all(outgoing, 'slab', split_axis=0, concat_axis=0, tiled=True)]
    ppermute x0 -> x14, starting transfers between devices: none -> 18.9 us  [swapped_with_each(): part = lax.ppermute(part, axis, [(d, d ^ mask) for d in range(ways)])]
    dynamic_update_slice x0 -> x14, local copies, waits for them, and re-layouts: none -> 10.1 us  [swapped_with_each(): lax.dynamic_update_slice_in_dim(full, part, (here ^ mask) * height, axis=...]
    all_to_all x1 -> x0, starting transfers between devices: 4.47 us -> none  [local(): lax.all_to_all(outgoing, 'slab', split_axis=0, concat_axis=0, tiled=True)]
    another operation x2 -> x4, local copies, waits for them, and re-layouts: 0.12 us -> 3.26 us
  transfers between devices with their start and end apart: 3 -> 16, of which waited for: 3 -> 11; matrix products, arithmetic and copies ran while one was open for 0% -> 3% of each run, Pallas kernels for 0% -> 0%
where the time goes in v1:
time: 314 us; the launch traced here: 311 us
  matrix products  90.5 us (29%)
  waiting for transfers between devices  79.6 us (25%)
  blocking collectives  54 us (17%)
  local copies, waits for them, and re-layouts  39.5 us (13%)
  starting transfers between devices  36.1 us (11%)
  other arithmetic  9.11 us (3%)
    dot_general x64, matrix products, advance(): jnp.dot(hidden, weight_rec, preferred_element_type=jnp.float32)  72.8 us
    all_to_all x2, blocking collectives, recur(): return lax.all_to_all(states, 'tm', split_axis=0, concat_axis=0, tiled=True)  54 us
    all_to_all x2, waiting for transfers between devices, local(): lax.all_to_all(grouped, 'tm', split_axis=0, concat_axis=0, tiled=True)  44.3 us
    ppermute x14, waiting for transfers between devices, swapped_with_each(): part = lax.ppermute(part, axis, [(d, d ^ mask) for d in range(ways)])  35.3 us
    ppermute x14, starting transfers between devices, swapped_with_each(): part = lax.ppermute(part, axis, [(d, d ^ mask) for d in range(ways)])  18.9 us
    all_to_all x2, starting transfers between devices, local(): lax.all_to_all(grouped, 'tm', split_axis=0, concat_axis=0, tiled=True)  17.3 us
    dynamic_update_slice x14, local copies, waits for them, and re-layouts, swapped_with_each(): lax.dynamic_update_slice_in_dim(full, part, (here ^ mask) * height, axis=...  10.1 us
    dot_general x2, matrix products, lstm_run(): jnp.dot(inputs.reshape(-1, feature_width), weight_in, preferred_element_t...  9.33 us
  transfers between devices with their start and end apart: 16, of which 11 were waited for; matrix products, arithmetic and copies ran while one was open for 3% of the time, Pallas kernels for 0%

profile of v1, /device:TPU:8, one launch (start us, length us, event | category | flops | bytes accessed | tf_op | source)
XLA Modules:
  0.0 311.0 jit_solution(689907701544148963)
XLA Ops:
  1.6 3.2 %gather_fusion = bf16[32,128,256]{2,1,0:T(8,128)(2,1)} fusion(bf16[12,128,256]{2,1,0:T(8,128)(2,1)} %bitcast.186, s32[1024]{0:T(1024)S(1)} %pad_clamp_fusion.1), kind=kCustom, calls=%fused_computation.clone | custom fusion | bytes 4194432 | tf_op jit(solution)/shard_map/jit(_take)/gather | solution.py:70
  11.0 3.0 collective-permute-start.3
  14.8 2.9 collective-permute-start.5
  23.8 8.0 %collective-permute-done.3 = bf16[1,4,128,256]{3,2,1,0:T(8,128)(2,1)S(1)} collective-permute-done((bf16[1,4,128,256]{3,2,1,0:T(8,128)(2,1)S(1)}, bf16[1,4,128,256]{3,2,1,0:T(8,128)(2,1)S(1)}, u32[]{:S(2)}, u32[]{:S(2)}) %collective-permute-start.3) | collective-permute-done | bytes 262176 | tf_op jit(solution)/shard_map/ppermute | solution.py:18
  32.5 4.1 %collective-permute-done.4 = bf16[1,4,128,256]{3,2,1,0:T(8,128)(2,1)S(1)} collective-permute-done((bf16[1,4,128,256]{3,2,1,0:T(8,128)(2,1)S(1)}, bf16[1,4,128,256]{3,2,1,0:T(8,128)(2,1)S(1)}, u32[]{:S(2)}, u32[]{:S(2)}) %collective-permute-start.4) | collective-permute-done | bytes 262176 | tf_op jit(solution)/shard_map/ppermute | solution.py:18
  38.1 3.2 %collective-permute-done.6 = bf16[1,4,128,256]{3,2,1,0:T(8,128)(2,1)S(1)} collective-permute-done((bf16[1,4,128,256]{3,2,1,0:T(8,128)(2,1)S(1)}, bf16[1,4,128,256]{3,2,1,0:T(8,128)(2,1)S(1)}, u32[]{:S(2)}, u32[]{:S(2)}) %collective-permute-start.6) | collective-permute-done | bytes 262176 | tf_op jit(solution)/shard_map/ppermute | solution.py:18
  46.5 3.4 %copy.12 = bf16[32,256,128]{1,0,2:T(8,128)(2,1)S(1)} copy(bf16[32,256,128]{2,1,0:T(8,128)(2,1)} %fusion.128) | data formatting | bytes 4194304 | tf_op jit(solution)/shard_map/kij,kjf->kif/dot_general | solution.py:76
  51.5 11.7 %all-to-all-start = ((bf16[32,48,256]{2,1,0:T(8,128)(2,1)}), bf16[32,48,256]{2,1,0:T(8,128)(2,1)S(1)}, u32[]{:S(2)}, u32[]{:S(2)}) async-start(bf16[32,48,256]{2,1,0:T(8,128)(2,1)} %bitcast.9), calls=%async_computation | async-start | bytes 1572864 | tf_op jit(solution)/shard_map/all_to_all | solution.py:89
  64.5 21.5 %all-to-all-done = bf16[32,48,256]{2,1,0:T(8,128)(2,1)S(1)} async-done(((bf16[32,48,256]{2,1,0:T(8,128)(2,1)}), bf16[32,48,256]{2,1,0:T(8,128)(2,1)S(1)}, u32[]{:S(2)}, u32[]{:S(2)}) %all-to-all-start) | async-done | bytes 786464 | tf_op jit(solution)/shard_map/all_to_all | solution.py:89
  86.0 4.7 %broadcast_add_fusion.1 = f32[32,48,1024]{2,1,0:T(8,128)} fusion(f32[1024]{0:T(1024)S(1)} %bitcast.199, bf16[32,48,256]{2,1,0:T(8,128)(2,1)S(1)} %all-to-all-done, bf16[2,256,1024]{2,1,0:T(8,128)(2,1)} %param.23), kind=kOutput, calls=%fused_computation.181 | convolution fusion | flops 806879232 | bytes 7606272 | tf_op jit(solution)/shard_map/dot_general | solution.py:25
  90.8 39.4 %while.30 = (s32[]{:T(128)}, bf16[48,256]{1,0:T(8,128)(2,1)S(1)}, f32[48,256]{1,0:T(8,128)S(1)}, bf16[8,4,48,256]{3,2,1,0:T(8,128)(2,1)S(1)}, f32[8,4,48,1024]{3...) while((s32[]{:T(128)}, bf16[48,256]{1,0:T(8,128)(2,1)S(1)}, ...), condition=%wide.region_1.0_spmd.clone, body=%wide.region_0.3_spmd.clone.sunk | while | flops 101965824 | bytes 5243068 | solution.py:43
  130.2 27.0 %all_to_all.20 = bf16[32,48,256]{2,1,0:T(8,128)(2,1)S(1)} all-to-all(bf16[32,48,256]{2,1,0:T(8,128)(2,1)S(1)} %bitcast.194), channel_id=1, replica_groups=mesh['tm'=32,'slab'=8] {'tm'}, dimensions={0} | all-to-all | bytes 1572864 | tf_op jit(solution)/shard_map/all_to_all | solution.py:86
  165.3 2.5 collective-permute-start.10
  168.4 2.8 collective-permute-start.12
  178.1 8.0 %collective-permute-done.10 = bf16[1,4,128,256]{3,2,1,0:T(8,128)(2,1)S(1)} collective-permute-done((bf16[1,4,128,256]{3,2,1,0:T(8,128)(2,1)S(1)}, bf16[1,4,128,256]{3,2,1,0:T(8,128)(2,1)S(1)}, u32[]{:S(2)}, u32[]{:S(2)}) %collective-permute-start.10) | collective-permute-done | bytes 262176 | tf_op jit(solution)/shard_map/ppermute | solution.py:18
  186.8 4.1 %collective-permute-done.11 = bf16[1,4,128,256]{3,2,1,0:T(8,128)(2,1)S(1)} collective-permute-done((bf16[1,4,128,256]{3,2,1,0:T(8,128)(2,1)S(1)}, bf16[1,4,128,256]{3,2,1,0:T(8,128)(2,1)S(1)}, u32[]{:S(2)}, u32[]{:S(2)}) %collective-permute-start.11) | collective-permute-done | bytes 262176 | tf_op jit(solution)/shard_map/ppermute | solution.py:18
  195.6 3.6 %gather_fusion.3 = bf16[32,128,256]{2,1,0:T(8,128)(2,1)} fusion(bf16[32,128,256]{2,1,0:T(8,128)(2,1)} %bitcast.18, s32[1024]{0:T(1024)S(1)} %pad_clamp_fusion), kind=kCustom, calls=%fused_computation.3.clone | custom fusion | bytes 4194432 | tf_op jit(solution)/shard_map/jit(_take)/gather | solution.py:75
  199.2 3.7 %fusion.126 = bf16[32,256,128]{2,1,0:T(8,128)(2,1)} fusion(bf16[32,128,256]{2,1,0:T(8,128)(2,1)} %gather_fusion.3, pred[32]{0:T(512)(128)(4,1)S(1)} %get-tuple-element.175, bf16[1,32,128,128]{3,2,1,0:T(8,128)(2,1)S(1)} %copy-done), kind=kOutput, calls=%fused_computation.182 | convolution fusion | flops 269484032 | bytes 5242912 | tf_op jit(solution)/shard_map/kij,kjf->kif/dot_general | solution.py:76
  202.9 4.6 %copy.13 = bf16[32,256,128]{1,0,2:T(8,128)(2,1)} copy(bf16[32,256,128]{2,1,0:T(8,128)(2,1)} %fusion.126) | data formatting | bytes 4194304 | tf_op jit(solution)/shard_map/kij,kjf->kif/dot_general | solution.py:76
  210.7 5.6 %all-to-all-start.2 = ((bf16[32,48,256]{2,1,0:T(8,128)(2,1)}), bf16[32,48,256]{2,1,0:T(8,128)(2,1)S(1)}, u32[]{:S(2)}, u32[]{:S(2)}) async-start(bf16[32,48,256]{2,1,0:T(8,128)(2,1)} %bitcast.20), calls=%async_computation.2 | async-start | bytes 1572864 | tf_op jit(solution)/shard_map/all_to_all | solution.py:89
  216.3 22.8 %all-to-all-done.2 = bf16[32,48,256]{2,1,0:T(8,128)(2,1)S(1)} async-done(((bf16[32,48,256]{2,1,0:T(8,128)(2,1)}), bf16[32,48,256]{2,1,0:T(8,128)(2,1)S(1)}, u32[]{:S(2)}, u32[]{:S(2)}) %all-to-all-start.2) | async-done | bytes 786464 | tf_op jit(solution)/shard_map/all_to_all | solution.py:89
  239.0 4.7 %broadcast_add_fusion = f32[32,48,1024]{2,1,0:T(8,128)} fusion(f32[1024]{0:T(1024)S(1)} %bitcast.198, bf16[32,48,256]{2,1,0:T(8,128)(2,1)S(1)} %all-to-all-done.2, bf16[2,256,1024]{2,1,0:T(8,128)(2,1)} %param.23), kind=kOutput, calls=%fused_computation.180 | convolution fusion | flops 806879232 | bytes 7606272 | tf_op jit(solution)/shard_map/dot_general | solution.py:25
  243.8 39.4 %while.31 = (s32[]{:T(128)}, bf16[48,256]{1,0:T(8,128)(2,1)S(1)}, f32[48,256]{1,0:T(8,128)S(1)}, bf16[8,4,48,256]{3,2,1,0:T(8,128)(2,1)S(1)}, f32[8,4,48,1024]{3...) while((s32[]{:T(128)}, bf16[48,256]{1,0:T(8,128)(2,1)S(1)}, ...), condition=%wide.region_3.6_spmd.clone, body=%wide.region_2.5_spmd.clone.sunk | while | flops 101965824 | bytes 5243068 | solution.py:43
  283.2 27.0 %all_to_all.21 = bf16[32,48,256]{2,1,0:T(8,128)(2,1)S(1)} all-to-all(bf16[32,48,256]{2,1,0:T(8,128)(2,1)S(1)} %bitcast.193), channel_id=1, replica_groups=mesh['tm'=32,'slab'=8] {'tm'}, dimensions={0} | all-to-all | bytes 1572864 | tf_op jit(solution)/shard_map/all_to_all | solution.py:86
  (215 shorter events, 126.9 us)
Async XLA Ops:
  0.0 44.3 %copy-start = (bf16[1,32,128,128]{3,2,1,0:T(8,128)(2,1)S(1)}, bf16[1,32,128,128]{3,2,1,0:T(8,128)(2,1)}, u32[]{:S(2)}) copy-start(bf16[1,32,128,128]{3,2,1,0:T(8,128)(2,1)} %param.22) | copy-start | bytes 3145732
  8.2 5.9 %copy-start.3 = (s32[1,32]{1,0:T(1,128)S(1)}, s32[1,32]{1,0:T(1,128)}, u32[]{:S(2)}) copy-start(s32[1,32]{1,0:T(1,128)} %param.20) | copy-start | bytes 388
  9.1 5.7 %collective-permute-start = (bf16[1,4,128,256]{3,2,1,0:T(8,128)(2,1)S(1)}, bf16[1,4,128,256]{3,2,1,0:T(8,128)(2,1)S(1)}, u32[]{:S(2)}, u32[]{:S(2)}) collective-permute-start(bf16[1,4,128,256]{3,2,1,0:T(8,128)(2,1)S(1)} %get-tuple-element.169), channel_id=1, source_target_pairs={{0,1},{1,0},{2,3},{3,2},{4,5},{5,4},{6,7},{7,6},{8,9},{9,8},{10,11... | collective-permute-start | bytes 786440 | tf_op jit(solution)/shard_map/ppermute | solution.py:18
  9.1 9.3 %collective-permute-start.1 = (bf16[1,4,128,256]{3,2,1,0:T(8,128)(2,1)S(1)}, bf16[1,4,128,256]{3,2,1,0:T(8,128)(2,1)S(1)}, u32[]{:S(2)}, u32[]{:S(2)}) collective-permute-start(bf16[1,4,128,256]{3,2,1,0:T(8,128)(2,1)S(1)} %get-tuple-element.168), channel_id=1, source_target_pairs={{0,2},{1,3},{2,0},{3,1},{4,6},{5,7},{6,4},{7,5},{8,10},{9,11},{10,... | collective-permute-start | bytes 786440 | tf_op jit(solution)/shard_map/ppermute | solution.py:18
  10.6 12.5 %collective-permute-start.2 = (bf16[1,4,128,256]{3,2,1,0:T(8,128)(2,1)S(1)}, bf16[1,4,128,256]{3,2,1,0:T(8,128)(2,1)S(1)}, u32[]{:S(2)}, u32[]{:S(2)}) collective-permute-start(bf16[1,4,128,256]{3,2,1,0:T(8,128)(2,1)S(1)} %get-tuple-element.167), channel_id=1, source_target_pairs={{0,3},{1,2},{2,1},{3,0},{4,7},{5,6},{6,5},{7,4},{8,11},{9,10},{10,... | collective-permute-start | bytes 786440 | tf_op jit(solution)/shard_map/ppermute | solution.py:18
  11.0 20.8 %collective-permute-start.3 = (bf16[1,4,128,256]{3,2,1,0:T(8,128)(2,1)S(1)}, bf16[1,4,128,256]{3,2,1,0:T(8,128)(2,1)S(1)}, u32[]{:S(2)}, u32[]{:S(2)}) collective-permute-start(bf16[1,4,128,256]{3,2,1,0:T(8,128)(2,1)S(1)} %get-tuple-element.166), channel_id=1, source_target_pairs={{0,4},{1,5},{2,6},{3,7},{4,0},{5,1},{6,2},{7,3},{8,12},{9,13},{10,... | collective-permute-start | bytes 786440 | tf_op jit(solution)/shard_map/ppermute | solution.py:18
  14.0 22.6 %collective-permute-start.4 = (bf16[1,4,128,256]{3,2,1,0:T(8,128)(2,1)S(1)}, bf16[1,4,128,256]{3,2,1,0:T(8,128)(2,1)S(1)}, u32[]{:S(2)}, u32[]{:S(2)}) collective-permute-start(bf16[1,4,128,256]{3,2,1,0:T(8,128)(2,1)S(1)} %get-tuple-element.165), channel_id=1, source_target_pairs={{0,5},{1,4},{2,7},{3,6},{4,1},{5,0},{6,3},{7,2},{8,13},{9,12},{10,... | collective-permute-start | bytes 786440 | tf_op jit(solution)/shard_map/ppermute | solution.py:18
  14.8 22.5 %collective-permute-start.5 = (bf16[1,4,128,256]{3,2,1,0:T(8,128)(2,1)S(1)}, bf16[1,4,128,256]{3,2,1,0:T(8,128)(2,1)S(1)}, u32[]{:S(2)}, u32[]{:S(2)}) collective-permute-start(bf16[1,4,128,256]{3,2,1,0:T(8,128)(2,1)S(1)} %get-tuple-element.164), channel_id=1, source_target_pairs={{0,6},{1,7},{2,4},{3,5},{4,2},{5,3},{6,0},{7,1},{8,14},{9,15},{10,... | collective-permute-start | bytes 786440 | tf_op jit(solution)/shard_map/ppermute | solution.py:18
  18.4 22.9 %collective-permute-start.6 = (bf16[1,4,128,256]{3,2,1,0:T(8,128)(2,1)S(1)}, bf16[1,4,128,256]{3,2,1,0:T(8,128)(2,1)S(1)}, u32[]{:S(2)}, u32[]{:S(2)}) collective-permute-start(bf16[1,4,128,256]{3,2,1,0:T(8,128)(2,1)S(1)} %get-tuple-element.163), channel_id=1, source_target_pairs={{0,7},{1,6},{2,5},{3,4},{4,3},{5,2},{6,1},{7,0},{8,15},{9,14},{10,... | collective-permute-start | bytes 786440 | tf_op jit(solution)/shard_map/ppermute | solution.py:18
  46.5 3.4 %copy-start.2 = (s32[1,32]{1,0:T(1,128)S(1)}, s32[1,32]{1,0:T(1,128)}, u32[]{:S(2)}) copy-start(s32[1,32]{1,0:T(1,128)} %param.19) | copy-start | bytes 388
  50.4 12.9 %copy-start.1 = (f32[2,1024]{1,0:T(2,128)S(1)}, f32[2,1024]{1,0:T(2,128)}, u32[]{:S(2)}) copy-start(f32[2,1024]{1,0:T(2,128)} %param.25) | copy-start | bytes 24580
  51.5 34.5 %all-to-all-start = ((bf16[32,48,256]{2,1,0:T(8,128)(2,1)}), bf16[32,48,256]{2,1,0:T(8,128)(2,1)S(1)}, u32[]{:S(2)}, u32[]{:S(2)}) async-start(bf16[32,48,256]{2,1,0:T(8,128)(2,1)} %bitcast.9), calls=%async_computation | async-start | bytes 1572864 | tf_op jit(solution)/shard_map/all_to_all | solution.py:89
  163.4 5.0 %collective-permute-start.7 = (bf16[1,4,128,256]{3,2,1,0:T(8,128)(2,1)S(1)}, bf16[1,4,128,256]{3,2,1,0:T(8,128)(2,1)S(1)}, u32[]{:S(2)}, u32[]{:S(2)}) collective-permute-start(bf16[1,4,128,256]{3,2,1,0:T(8,128)(2,1)S(1)} %get-tuple-element.161), channel_id=1, source_target_pairs={{0,1},{1,0},{2,3},{3,2},{4,5},{5,4},{6,7},{7,6},{8,9},{9,8},{10,11... | collective-permute-start | bytes 786440 | tf_op jit(solution)/shard_map/ppermute | solution.py:18
  163.4 9.1 %collective-permute-start.8 = (bf16[1,4,128,256]{3,2,1,0:T(8,128)(2,1)S(1)}, bf16[1,4,128,256]{3,2,1,0:T(8,128)(2,1)S(1)}, u32[]{:S(2)}, u32[]{:S(2)}) collective-permute-start(bf16[1,4,128,256]{3,2,1,0:T(8,128)(2,1)S(1)} %get-tuple-element.160), channel_id=1, source_target_pairs={{0,2},{1,3},{2,0},{3,1},{4,6},{5,7},{6,4},{7,5},{8,10},{9,11},{10,... | collective-permute-start | bytes 786440 | tf_op jit(solution)/shard_map/ppermute | solution.py:18
  164.0 13.4 %collective-permute-start.9 = (bf16[1,4,128,256]{3,2,1,0:T(8,128)(2,1)S(1)}, bf16[1,4,128,256]{3,2,1,0:T(8,128)(2,1)S(1)}, u32[]{:S(2)}, u32[]{:S(2)}) collective-permute-start(bf16[1,4,128,256]{3,2,1,0:T(8,128)(2,1)S(1)} %get-tuple-element.159), channel_id=1, source_target_pairs={{0,3},{1,2},{2,1},{3,0},{4,7},{5,6},{6,5},{7,4},{8,11},{9,10},{10,... | collective-permute-start | bytes 786440 | tf_op jit(solution)/shard_map/ppermute | solution.py:18
  165.3 20.8 %collective-permute-start.10 = (bf16[1,4,128,256]{3,2,1,0:T(8,128)(2,1)S(1)}, bf16[1,4,128,256]{3,2,1,0:T(8,128)(2,1)S(1)}, u32[]{:S(2)}, u32[]{:S(2)}) collective-permute-start(bf16[1,4,128,256]{3,2,1,0:T(8,128)(2,1)S(1)} %get-tuple-element.158), channel_id=1, source_target_pairs={{0,4},{1,5},{2,6},{3,7},{4,0},{5,1},{6,2},{7,3},{8,12},{9,13},{10,... | collective-permute-start | bytes 786440 | tf_op jit(solution)/shard_map/ppermute | solution.py:18
  167.8 23.1 %collective-permute-start.11 = (bf16[1,4,128,256]{3,2,1,0:T(8,128)(2,1)S(1)}, bf16[1,4,128,256]{3,2,1,0:T(8,128)(2,1)S(1)}, u32[]{:S(2)}, u32[]{:S(2)}) collective-permute-start(bf16[1,4,128,256]{3,2,1,0:T(8,128)(2,1)S(1)} %get-tuple-element.157), channel_id=1, source_target_pairs={{0,5},{1,4},{2,7},{3,6},{4,1},{5,0},{6,3},{7,2},{8,13},{9,12},{10,... | collective-permute-start | bytes 786440 | tf_op jit(solution)/shard_map/ppermute | solution.py:18
  168.4 23.2 %collective-permute-start.12 = (bf16[1,4,128,256]{3,2,1,0:T(8,128)(2,1)S(1)}, bf16[1,4,128,256]{3,2,1,0:T(8,128)(2,1)S(1)}, u32[]{:S(2)}, u32[]{:S(2)}) collective-permute-start(bf16[1,4,128,256]{3,2,1,0:T(8,128)(2,1)S(1)} %get-tuple-element.156), channel_id=1, source_target_pairs={{0,6},{1,7},{2,4},{3,5},{4,2},{5,3},{6,0},{7,1},{8,14},{9,15},{10,... | collective-permute-start | bytes 786440 | tf_op jit(solution)/shard_map/ppermute | solution.py:18
  172.5 22.3 %collective-permute-start.13 = (bf16[1,4,128,256]{3,2,1,0:T(8,128)(2,1)S(1)}, bf16[1,4,128,256]{3,2,1,0:T(8,128)(2,1)S(1)}, u32[]{:S(2)}, u32[]{:S(2)}) collective-permute-start(bf16[1,4,128,256]{3,2,1,0:T(8,128)(2,1)S(1)} %get-tuple-element.155), channel_id=1, source_target_pairs={{0,7},{1,6},{2,5},{3,4},{4,3},{5,2},{6,1},{7,0},{8,15},{9,14},{10,... | collective-permute-start | bytes 786440 | tf_op jit(solution)/shard_map/ppermute | solution.py:18
  210.7 28.4 %all-to-all-start.2 = ((bf16[32,48,256]{2,1,0:T(8,128)(2,1)}), bf16[32,48,256]{2,1,0:T(8,128)(2,1)S(1)}, u32[]{:S(2)}, u32[]{:S(2)}) async-start(bf16[32,48,256]{2,1,0:T(8,128)(2,1)} %bitcast.20), calls=%async_computation.2 | async-start | bytes 1572864 | tf_op jit(solution)/shard_map/all_to_all | solution.py:89
